TPU v7x, 256 devices: a whole 4x4x8 slice. The times are simulated.
256 devices in a mesh: frames: 4 (over z_hi), states: 64 (over z_lo, y, x, core).
Axes of the slice: x: 4, y: 4, z: 8 (z_hi: 4, z_lo: 2; z = z_hi * 2 + z_lo), core: 2. Of those that a mesh axis runs over, the one named last changes fastest.
Arguments:
- features: bfloat16 [16384, 1024], P('states', 'frames'), may hold values from -10 to 10
- state_ids: int32 [16384, 32], P('states'), may hold values from 0 to 6143, as said below
- weights: float32 [16384, 32], P('states'), may hold values from 0.05 to 1
Outputs:
- means: bfloat16 [6144, 1024], P(None, 'frames')
- precisions: bfloat16 [6144, 1024], P(None, 'frames')
- frame_score: float32 [16384], P('states')
Inputs may be any that keep to these rules, and one draw needn't show every extreme that they name: `state_ids`: each row names 32 different states; every state is named by some row.
All inputs are finite; a program needn't handle non-finite values.
Results may differ from a plain program's by a relative error of at most 0.0034.
Values may be sent and summed in bfloat16 or wider, within the bound.
A program may use at most 128 MiB of HBM per device.

v0:
```python
import jax
import jax.numpy as jnp
from jax import lax
from jax.sharding import PartitionSpec as P

D = 1024
STATE_DEV = 96
variance_floor = 0.25


def copy_for_each(shard, axis):
    copies = jnp.broadcast_to(shard, (lax.axis_size(axis), *shard.shape))
    return lax.all_to_all(copies, axis, split_axis=0, concat_axis=0, tiled=True)


def taken_together(shard, axis):
    everything = copy_for_each(shard, axis)
    return jnp.sum(everything, axis=0)


def refresh(first, second, counts):
    mean_value = first / counts
    variance = jnp.maximum(second / counts - mean_value * mean_value, variance_floor)
    return (mean_value.astype(jnp.bfloat16), (1.0 / variance).astype(jnp.bfloat16))


def per_device(features, state_ids, weights):
    rows_here, local_width = features.shape
    group_size = lax.axis_size("states")
    total_states = STATE_DEV * group_size
    row_index = jnp.arange(rows_here, dtype=jnp.int32)[:, None]
    rounded = weights.astype(jnp.bfloat16)
    posterior = (
        jnp.zeros((rows_here, total_states), jnp.bfloat16).at[row_index, state_ids].add(rounded)
    )
    values = features.astype(jnp.float32)
    squares = (values * values).astype(jnp.bfloat16)
    blocked = posterior.reshape(rows_here, group_size, STATE_DEV)
    routed = lax.all_to_all(blocked, "states", split_axis=1, concat_axis=0, tiled=True)
    routed = routed.reshape(rows_here * group_size, STATE_DEV)
    owned_counts = jnp.sum(routed, axis=0, dtype=jnp.float32)
    piece = lax.all_gather(features, "states", axis=0, tiled=True)
    piece_f = piece.astype(jnp.float32)
    piece_sq = (piece_f * piece_f).astype(jnp.bfloat16)
    joined = jnp.concatenate([piece, piece_sq], axis=1)
    owned_sums = lax.dot_general(
        routed, joined, (((0,), (0,)), ((), ())), preferred_element_type=jnp.float32
    )
    mean_rows, prec_rows = refresh(
        owned_sums[:, :local_width], owned_sums[:, local_width:], owned_counts[:, None]
    )
    packed = lax.all_gather(
        jnp.concatenate([mean_rows, prec_rows], axis=1), "states", axis=0, tiled=True
    )
    means = packed[:, :local_width]
    precisions = packed[:, local_width:]
    mean_f = means.astype(jnp.float32)
    prec_f = precisions.astype(jnp.float32)
    product = (mean_f * prec_f).astype(jnp.bfloat16)
    constant_term = jnp.sum(mean_f * product.astype(jnp.float32) - jnp.log(prec_f), axis=1)
    lookup_table = jnp.concatenate([precisions, product], axis=1)
    weight_f = rounded.astype(jnp.float32)
    blended = jnp.dot(posterior, lookup_table, preferred_element_type=jnp.float32)
    quadratic = jnp.sum(
        squares.astype(jnp.float32) * blended[:, :local_width]
        - 2.0 * values * blended[:, local_width:],
        axis=1,
    )
    quadratic = quadratic + jnp.sum(weight_f * constant_term[state_ids], axis=1)
    summed = taken_together(quadratic, "frames")
    weight_sum = jnp.sum(weight_f, axis=1)
    frame_score = -0.5 * summed / (D * weight_sum)
    return (means, precisions, frame_score)


def solution(mesh):
    return jax.shard_map(
        per_device,
        mesh=mesh,
        in_specs=(P("states", "frames"), P("states", None), P("states", None)),
        out_specs=(P(None, "frames"), P(None, "frames"), P("states")),
        check_vma=False,
    )
```

profile of v0, /device:TPU:1, one launch (start us, length us, event | category | flops | bytes accessed | tf_op | source)
XLA Modules:
  0.0 357.5 jit_solution(10742842729083389817)
XLA Ops:
  7.2 0.0 all-gather.3.cloned.1.call-start
  7.2 0.7 all-gather.3.cloned.1.call-update
  7.9 0.0 all-gather.5.cloned.1.call-start
  7.9 0.9 copy.20
  8.8 0.1 reshape.37
  8.9 0.8 compare_select_fusion
  9.7 0.7 multiply_reduce_fusion
  10.4 0.7 and_reduce_fusion
  11.2 0.1 copy.19
  11.3 0.1 reshape.35
  11.4 57.8 %scatter_custom_fusion = bf16[1572864]{0:T(1024)(128)(2,1)S(1)} fusion(s32[8192]{0:T(1024)S(1)} %reshape.35, bf16[8192]{0:T(1024)(128)(2,1)S(1)} %reshape.37, bf16[]{:T(256)} %constant.9.clone.1), kind=kCustom, calls=%fused_computation.18 | custom fusion | flops 8192 | bytes 3145730
  69.2 4.0 %reshape.20 = bf16[256,64,96]{2,1,0:T(8,128)(2,1)} reshape(bf16[1572864]{0:T(1024)(128)(2,1)S(1)} %scatter_custom_fusion) | data formatting | bytes 6291456 | tf_op jit(solution)/shard_map/reshape | solution.py:38
  73.2 6.5 %copy.21 = bf16[256,64,96]{0,2,1:T(8,128)(2,1)} copy(bf16[256,64,96]{2,1,0:T(8,128)(2,1)} %reshape.20) | data formatting | bytes 6291456 | tf_op jit(solution)/shard_map/reshape | solution.py:38
  79.8 53.9 %all_to_all.21 = bf16[256,64,96]{0,2,1:T(8,128)(2,1)S(1)} all-to-all(bf16[256,64,96]{0,2,1:T(8,128)(2,1)} %copy.21), channel_id=1, replica_groups=mesh['frames'=4,'states'=64] {'states'}, dimensions={1} | all-to-all | bytes 6291456 | tf_op jit(solution)/shard_map/all_to_all | solution.py:39
  133.7 1.9 copy.26
  135.6 0.5 convert_reduce_fusion
  136.2 18.2 %all-gather.3.cloned.1.call-done = bf16[16384,256]{1,0:T(8,128)(2,1)} async-done(((bf16[256,256]{1,0:T(8,128)(2,1)}), bf16[16384,256]{1,0:T(8,128)(2,1)}) %all-gather.3.cloned.1.call-update) | async-done | bytes 8388624 | tf_op jit(solution)/shard_map/all_gather | solution.py:42
  154.3 0.0 copy-start
  154.3 0.0 copy-start.2
  154.3 8.7 %multiply_convert_fusion = bf16[16384,256]{1,0:T(8,128)(2,1)} fusion(bf16[16384,256]{1,0:T(8,128)(2,1)} %all-gather.3.cloned.1.call-done), kind=kLoop, calls=%fused_computation.6 | loop fusion | flops 12582912 | bytes 16777216 | tf_op jit(solution)/shard_map/convert_element_type | solution.py:44
  163.1 0.0 copy-done
  163.1 1.1 copy-done.2
  164.2 8.5 %fusion = f32[96,512]{1,0:T(8,128)S(1)} fusion(bf16[16384,96]{0,1:T(8,128)(2,1)S(1)} %bitcast.16, bf16[16384,256]{1,0:T(8,128)(2,1)} %multiply_convert_fusion, bf16[16384,256]{1,0:T(8,128)(2,1)S(1)} %copy-done), kind=kOutput, calls=%fused_computation.2 | convolution fusion | flops 1644167168 | bytes 20119552 | tf_op jit(solution)/shard_map/dot_general | solution.py:46
  172.7 0.1 fusion.22
  172.8 0.6 pad_maximum_fusion
  173.5 0.0 all-gather.5.cloned.1.call-update
  173.5 2.9 reshape.25
  176.4 0.1 copy.23
  176.5 0.1 reshape.29
  176.6 0.0 copy-start.1
  176.6 108.3 %all-gather.5.cloned.1.call-done = bf16[6144,512]{1,0:T(8,128)(2,1)} async-done(((bf16[96,512]{1,0:T(8,128)(2,1)}), bf16[6144,512]{1,0:T(8,128)(2,1)}) %all-gather.5.cloned.1.call-update) | async-done | bytes 6291472 | tf_op jit(solution)/shard_map/all_gather | solution.py:52
  284.9 4.9 %fusion.5 = (f32[6144]{0:T(1024)S(1)}, bf16[6144,256]{1,0:T(8,128)(2,1)S(1)}, bf16[6144,256]{1,0:T(8,128)(2,1)S(1)}, bf16[6144,256]{1,0:T(8,128)(2,1)}) fusion(bf16[6144,512]{1,0:T(8,128)(2,1)} %all-gather.5.cloned.1.call-done), kind=kLoop, calls=%fused_computation.11 | loop fusion | flops 12576768 | bytes 15753216 | tf_op jit(solution)/shard_map/reduce_sum | solution.py:60
  289.8 0.0 copy-start.3
  289.8 0.0 copy-done.1
  289.8 0.0 copy-start.4
  289.8 1.8 fusion.7
  291.6 0.0 copy-done.3
  291.7 0.0 copy-done.4
  291.7 0.1 fusion.16
  291.8 45.5 %gather_fusion = f32[8192]{0:T(1024)S(1)} fusion(f32[6144]{0:T(1024)S(1)} %get-tuple-element.5, s32[8192]{0:T(1024)S(1)} %broadcast_clamp_fusion), kind=kCustom, calls=%fused_computation | custom fusion | bytes 98304 | tf_op jit(solution)/shard_map/gather | solution.py:69
  337.3 0.1 reshape.28
  337.4 0.2 fusion.17
  337.6 12.5 %all_to_all.22 = f32[4,1,256]{2,1,0:T(1,128)S(1)} all-to-all(f32[4,1,256]{2,1,0:T(1,128)S(1)} %broadcast_in_dim.20), channel_id=1, replica_groups=mesh['frames'=4,'states'=64] {'frames'}, dimensions={0} | all-to-all | bytes 8192 | tf_op jit(solution)/shard_map/all_to_all | solution.py:13
  350.1 0.6 multiply_divide_fusion
  (6 shorter events, 0.0 us)
Async XLA Ops:
  7.2 147.2 %all-gather.3.cloned.1.call-start = ((), (), s32[]{:S(2)}) async-start(), calls=%async_computation.2 | async-start | bytes 8519680 | tf_op jit(solution)/shard_map/all_gather | solution.py:42
  7.9 277.0 %all-gather.5.cloned.1.call-start = ((), (), s32[]{:S(2)}) async-start(), calls=%async_computation.3 | async-start | bytes 6389760 | tf_op jit(solution)/shard_map/all_gather | solution.py:52
  154.3 8.7 %copy-start = (bf16[16384,256]{1,0:T(8,128)(2,1)S(1)}, bf16[16384,256]{1,0:T(8,128)(2,1)}, u32[]{:S(2)}) copy-start(bf16[16384,256]{1,0:T(8,128)(2,1)} %all-gather.3.cloned.1.call-done) | copy-start | bytes 25165828
  154.3 9.8 %copy-start.2 = (bf16[12,8,64,256]{3,1,2,0:T(8,128)(2,1)S(1)}, bf16[12,8,64,256]{3,1,2,0:T(8,128)(2,1)}, u32[]{:S(2)}) copy-start(bf16[12,8,64,256]{3,1,2,0:T(8,128)(2,1)} %copy.26) | copy-start | bytes 9437188
  176.6 113.2 %copy-start.1 = (bf16[256,6144]{1,0:T(8,128)(2,1)S(1)}, bf16[256,6144]{1,0:T(8,128)(2,1)}, u32[]{:S(2)}) copy-start(bf16[256,6144]{1,0:T(8,128)(2,1)} %reshape.25) | copy-start | bytes 9437188
  289.8 1.9 copy-start.3
  289.8 1.9 copy-start.4
Sparse Core Ops, SparseCore 0:
  9.8 144.4 all-gather.2
  173.6 111.2 all-gather.4
where the time goes:
time: 358 us
  waiting for transfers between devices  127 us (35%)
  other arithmetic  75.8 us (21%)
  blocking collectives  66.4 us (19%)
  local copies, waits for them, and re-layouts  63.5 us (18%)
  between operations  14.2 us (4%)
  matrix products  10.4 us (3%)
    all_gather x1, waiting for transfers between devices, per_device(): lax.all_gather(jnp.concatenate([mean_rows, prec_rows], axis=1), 'states',...  108 us
    unnamed x4, other arithmetic  59.3 us
    all_to_all x1, blocking collectives, per_device(): lax.all_to_all(blocked, 'states', split_axis=1, concat_axis=0, tiled=True)  53.9 us
    gather x2, local copies, waits for them, and re-layouts, per_device(): quadratic = quadratic + jnp.sum(weight_f * constant_term[state_ids], axis=1)  45.6 us
    all_gather x1, waiting for transfers between devices, per_device(): piece = lax.all_gather(features, 'states', axis=0, tiled=True)  18.2 us
    all_to_all x1, blocking collectives, copy_for_each(): return lax.all_to_all(copies, axis, split_axis=0, concat_axis=0, tiled=True)  12.5 us
    reshape x2, local copies, waits for them, and re-layouts, per_device(): blocked = posterior.reshape(rows_here, group_size, STATE_DEV)  10.5 us
    convert_element_type x1, other arithmetic, per_device(): piece_sq = (piece_f * piece_f).astype(jnp.bfloat16)  8.71 us
  transfers between devices with their start and end apart: 2, of which 2 were waited for; matrix products, arithmetic and copies ran while one was open for 22% of the time, Pallas kernels for 0%

commit v1 on v0

--- a/solution.py
+++ b/solution.py
@@ -49,8 +49,14 @@
     mean_rows, prec_rows = refresh(
         owned_sums[:, :local_width], owned_sums[:, local_width:], owned_counts[:, None]
     )
-    packed = lax.all_gather(
-        jnp.concatenate([mean_rows, prec_rows], axis=1), "states", axis=0, tiled=True
+    packed = jnp.concatenate(
+        lax.all_to_all(
+            jnp.stack([jnp.concatenate([mean_rows, prec_rows], axis=1)] * lax.axis_size("states")),
+            "states",
+            0,
+            0,
+        ),
+        axis=0,
     )
     means = packed[:, :local_width]
     precisions = packed[:, local_width:]

time: 358 us -> 346 us (0.966)
  the two profiles are of different devices: /device:TPU:1 before, /device:TPU:8 now
where the time goes in v1:
time: 346 us; the launch traced here: 345 us
  waiting for transfers between devices  104 us (30%)
  other arithmetic  75.3 us (22%)
  blocking collectives  66.9 us (19%)
  local copies, waits for them, and re-layouts  66.8 us (19%)
  between operations  14.2 us (4%)
  matrix products  10.4 us (3%)
  starting transfers between devices  7.26 us (2%)
    all_to_all x1, waiting for transfers between devices, per_device(): lax.all_to_all(jnp.stack([jnp.concatenate([mean_rows, prec_rows], axis=1)...  84.1 us
    unnamed x4, other arithmetic  59.3 us
    all_to_all x1, blocking collectives, per_device(): lax.all_to_all(blocked, 'states', split_axis=1, concat_axis=0, tiled=True)  53.7 us
    gather x2, local copies, waits for them, and re-layouts, per_device(): quadratic = quadratic + jnp.sum(weight_f * constant_term[state_ids], axis=1)  45.6 us
    all_gather x1, waiting for transfers between devices, per_device(): piece = lax.all_gather(features, 'states', axis=0, tiled=True)  19.4 us
    all_to_all x1, blocking collectives, copy_for_each(): return lax.all_to_all(copies, axis, split_axis=0, concat_axis=0, tiled=True)  13.2 us
    reshape x2, local copies, waits for them, and re-layouts, per_device(): blocked = posterior.reshape(rows_here, group_size, STATE_DEV)  10.5 us
    convert_element_type x1, other arithmetic, per_device(): piece_sq = (piece_f * piece_f).astype(jnp.bfloat16)  8.71 us
  transfers between devices with their start and end apart: 2, of which 2 were waited for; matrix products, arithmetic and copies ran while one was open for 22% of the time, Pallas kernels for 0%

profile of v1, /device:TPU:8, one launch (start us, length us, event | category | flops | bytes accessed | tf_op | source)
XLA Modules:
  0.0 345.0 jit_solution(125567289840019530)
XLA Ops:
  7.2 0.0 all-gather.2.cloned.1.call-start
  7.2 0.7 all-gather.2.cloned.1.call-update
  7.9 0.9 copy.20
  8.8 0.1 reshape.43
  8.9 0.8 compare_select_fusion
  9.7 0.7 multiply_reduce_fusion
  10.4 0.7 and_reduce_fusion
  11.1 0.1 copy.19
  11.2 0.1 reshape.41
  11.3 57.8 %scatter_custom_fusion = bf16[1572864]{0:T(1024)(128)(2,1)S(1)} fusion(s32[8192]{0:T(1024)S(1)} %reshape.41, bf16[8192]{0:T(1024)(128)(2,1)S(1)} %reshape.43, bf16[]{:T(256)} %constant.9.clone.1), kind=kCustom, calls=%fused_computation.18 | custom fusion | flops 8192 | bytes 3145730
  69.2 4.0 %reshape.25 = bf16[256,64,96]{2,1,0:T(8,128)(2,1)} reshape(bf16[1572864]{0:T(1024)(128)(2,1)S(1)} %scatter_custom_fusion) | data formatting | bytes 6291456 | tf_op jit(solution)/shard_map/reshape | solution.py:38
  73.2 6.5 %copy.21 = bf16[256,64,96]{0,2,1:T(8,128)(2,1)} copy(bf16[256,64,96]{2,1,0:T(8,128)(2,1)} %reshape.25) | data formatting | bytes 6291456 | tf_op jit(solution)/shard_map/reshape | solution.py:38
  79.7 53.7 %all_to_all.26 = bf16[256,64,96]{0,2,1:T(8,128)(2,1)S(1)} all-to-all(bf16[256,64,96]{0,2,1:T(8,128)(2,1)} %copy.21), channel_id=1, replica_groups=mesh['frames'=4,'states'=64] {'states'}, dimensions={1} | all-to-all | bytes 6291456 | tf_op jit(solution)/shard_map/all_to_all | solution.py:39
  133.4 1.9 copy.26
  135.3 0.5 convert_reduce_fusion
  135.9 19.4 %all-gather.2.cloned.1.call-done = bf16[16384,256]{1,0:T(8,128)(2,1)} async-done(((bf16[256,256]{1,0:T(8,128)(2,1)}), bf16[16384,256]{1,0:T(8,128)(2,1)}) %all-gather.2.cloned.1.call-update) | async-done | bytes 8388624 | tf_op jit(solution)/shard_map/all_gather | solution.py:42
  155.2 0.0 copy-start
  155.2 0.0 copy-start.2
  155.2 8.7 %multiply_convert_fusion = bf16[16384,256]{1,0:T(8,128)(2,1)} fusion(bf16[16384,256]{1,0:T(8,128)(2,1)} %all-gather.2.cloned.1.call-done), kind=kLoop, calls=%fused_computation.6 | loop fusion | flops 12582912 | bytes 16777216 | tf_op jit(solution)/shard_map/convert_element_type | solution.py:44
  163.9 0.0 copy-done
  163.9 1.1 copy-done.2
  165.0 8.5 %fusion = f32[96,512]{1,0:T(8,128)S(1)} fusion(bf16[16384,96]{0,1:T(8,128)(2,1)S(1)} %bitcast.17, bf16[16384,256]{1,0:T(8,128)(2,1)} %multiply_convert_fusion, bf16[16384,256]{1,0:T(8,128)(2,1)S(1)} %copy-done), kind=kOutput, calls=%fused_computation.2 | convolution fusion | flops 1644167168 | bytes 20119552 | tf_op jit(solution)/shard_map/dot_general | solution.py:46
  173.6 0.1 fusion.22
  173.7 3.4 stack.2
  177.1 7.2 %all-to-all-start.1 = ((bf16[64,96,512]{2,1,0:T(8,128)(2,1)}), bf16[64,96,512]{2,1,0:T(8,128)(2,1)}, u32[]{:S(2)}, u32[]{:S(2)}) async-start(bf16[64,96,512]{2,1,0:T(8,128)(2,1)} %stack.2), calls=%async_computation.1 | async-start | bytes 12582912 | tf_op jit(solution)/shard_map/all_to_all | solution.py:53
  184.4 2.8 reshape.31
  187.2 0.1 copy.23
  187.3 0.1 reshape.35
  187.4 84.1 %all-to-all-done.1 = bf16[64,96,512]{2,1,0:T(8,128)(2,1)} async-done(((bf16[64,96,512]{2,1,0:T(8,128)(2,1)}), bf16[64,96,512]{2,1,0:T(8,128)(2,1)}, u32[]{:S(2)}, u32[]{:S(2)}) %all-to-all-start.1) | async-done | bytes 6291488 | tf_op jit(solution)/shard_map/all_to_all | solution.py:53
  271.6 0.0 copy-start.1
  271.6 5.0 %fusion.5 = (f32[6144]{0:T(1024)S(1)}, bf16[6144,256]{1,0:T(8,128)(2,1)S(1)}, bf16[6144,256]{1,0:T(8,128)(2,1)S(1)}, bf16[6144,256]{1,0:T(8,128)(2,1)}) fusion(bf16[6144,512]{1,0:T(8,128)(2,1)} %bitcast.4), kind=kLoop, calls=%fused_computation.11 | loop fusion | flops 12576768 | bytes 15753216 | tf_op jit(solution)/shard_map/reduce_sum | solution.py:66
  276.6 0.0 copy-start.3
  276.6 0.0 copy-done.1
  276.6 0.0 copy-start.4
  276.6 1.8 fusion.7
  278.4 0.0 copy-done.3
  278.4 0.0 copy-done.4
  278.4 0.1 fusion.16
  278.6 45.5 %gather_fusion = f32[8192]{0:T(1024)S(1)} fusion(f32[6144]{0:T(1024)S(1)} %get-tuple-element.5, s32[8192]{0:T(1024)S(1)} %broadcast_clamp_fusion), kind=kCustom, calls=%fused_computation | custom fusion | bytes 98304 | tf_op jit(solution)/shard_map/gather | solution.py:75
  324.1 0.1 reshape.34
  324.2 0.2 fusion.17
  324.4 13.2 %all_to_all.27 = f32[4,1,256]{2,1,0:T(1,128)S(1)} all-to-all(f32[4,1,256]{2,1,0:T(1,128)S(1)} %broadcast_in_dim.20), channel_id=1, replica_groups=mesh['frames'=4,'states'=64] {'frames'}, dimensions={0} | all-to-all | bytes 8192 | tf_op jit(solution)/shard_map/all_to_all | solution.py:13
  337.6 0.6 multiply_divide_fusion
  (7 shorter events, 0.1 us)
Async XLA Ops:
  7.2 148.1 %all-gather.2.cloned.1.call-start = ((), (), s32[]{:S(2)}) async-start(), calls=%async_computation.3 | async-start | bytes 8519680 | tf_op jit(solution)/shard_map/all_gather | solution.py:42
  155.2 8.7 %copy-start = (bf16[16384,256]{1,0:T(8,128)(2,1)S(1)}, bf16[16384,256]{1,0:T(8,128)(2,1)}, u32[]{:S(2)}) copy-start(bf16[16384,256]{1,0:T(8,128)(2,1)} %all-gather.2.cloned.1.call-done) | copy-start | bytes 25165828
  155.2 9.8 %copy-start.2 = (bf16[12,8,64,256]{3,1,2,0:T(8,128)(2,1)S(1)}, bf16[12,8,64,256]{3,1,2,0:T(8,128)(2,1)}, u32[]{:S(2)}) copy-start(bf16[12,8,64,256]{3,1,2,0:T(8,128)(2,1)} %copy.26) | copy-start | bytes 9437188
  177.1 94.4 %all-to-all-start.1 = ((bf16[64,96,512]{2,1,0:T(8,128)(2,1)}), bf16[64,96,512]{2,1,0:T(8,128)(2,1)}, u32[]{:S(2)}, u32[]{:S(2)}) async-start(bf16[64,96,512]{2,1,0:T(8,128)(2,1)} %stack.2), calls=%async_computation.1 | async-start | bytes 12582912 | tf_op jit(solution)/shard_map/all_to_all | solution.py:53
  271.6 5.0 %copy-start.1 = (bf16[256,6144]{1,0:T(8,128)(2,1)S(1)}, bf16[256,6144]{1,0:T(8,128)(2,1)}, u32[]{:S(2)}) copy-start(bf16[256,6144]{1,0:T(8,128)(2,1)} %reshape.31) | copy-start | bytes 9437188
  276.6 1.8 copy-start.3
  276.6 1.8 copy-start.4
Sparse Core Ops, SparseCore 0:
  9.8 145.3 all-gather.1
